TPU v7x, 32 devices: a whole 2x2x4 slice. The times are simulated.
32 devices in a mesh: streams: 2 (over y), span: 4 (over z), head: 2 (over x), seq: 2 (over core).
Axes of the slice: x: 2, y: 2, z: 4, core: 2. Of those that a mesh axis runs over, the one named last changes fastest.
Arguments:
- query_rows: bfloat16 [4096, 1280], P(('streams', 'span', 'seq'), 'head'), parts along dimension 0, may hold values from -100 to 100
- key_rows: bfloat16 [4096, 1280], P(('streams', 'span', 'seq'), 'head'), parts along dimension 0, may hold values from -5 to 5
- value_rows: bfloat16 [4096, 1280], P(('streams', 'span', 'seq'), 'head'), parts along dimension 0, may hold values from -6 to 6
- out_weight: bfloat16 [1280, 5120], P('head', 'seq'), may hold values from -0.59765625 to 0.59765625
- gate_table: float32 [4, 5120], P(None, 'head'), may hold values from 0.5 to 2
- step_index: int32 [8], P('streams'), parts along dimension 0, may hold values from 0 to 3
- block_mask: int32 [8, 4], P('streams'), parts along dimension 0, may hold values from 0 to 1, as said below
Outputs:
- gated_update: bfloat16 [4096, 5120], P(('streams', 'span', 'seq'), 'head'), parts along dimension 0
There are 2 independent parts, one for each index of `streams`. A program takes and returns all parts, laid end to end along the dimension named above; an argument that names none is the same for every part. Nothing has to cross between parts.
Inputs may be any that keep to these rules, and one draw needn't show every extreme that they name: block_mask[c, c] = 1 and block_mask[c, e] = 0 for e > c; entries below the diagonal are 0 or 1.
All inputs are finite; a program needn't handle non-finite values.
Results may differ from a plain program's by a relative error of at most 0.017.
Values may be sent and summed in bfloat16 or wider, within the bound.
No kernel may reach another device: no remote copies, remote signals or barrier semaphores. Data moves between devices by JAX's collectives and lax.ppermute only.
A program may use at most 192 MiB of HBM per device.

v0:
```python
import math
import jax
import jax.numpy as jnp
from jax import lax
from jax.sharding import PartitionSpec as P

HD = 128
NEG_FLOOR = -1e30


def on_device(query_rows, key_rows, value_rows, out_weight, gate_table, step_index, block_mask):
    tok_rows = query_rows.shape[0]
    heads_here = query_rows.shape[1] // HD
    group_count = lax.axis_size("span")
    span_tok = tok_rows * lax.axis_size("seq")
    my_span = lax.axis_index("span")
    group_ids = jnp.arange(group_count, dtype=jnp.int32)
    mask_row = jnp.sum(jnp.where(group_ids[:, None] == my_span, block_mask, 0), axis=0)
    query_three = query_rows.reshape(tok_rows, heads_here, HD)
    score_scale = 1.0 / math.sqrt(HD)
    run_max = jnp.full((heads_here, tok_rows), NEG_FLOOR, jnp.float32)
    key_part = lax.all_gather(key_rows, ("span", "seq"), axis=0, tiled=True)
    value_part = lax.all_gather(value_rows, ("span", "seq"), axis=0, tiled=True)
    piece_rows = key_part.shape[0]
    key_group = jnp.arange(piece_rows, dtype=jnp.int32) // span_tok
    visible = (
        jnp.sum(jnp.where(key_group[:, None] == group_ids[None, :], mask_row[None, :], 0), axis=1)
        == 1
    )
    scores = (
        jnp.einsum(
            "thd,khd->htk",
            query_three,
            key_part.reshape(piece_rows, heads_here, HD),
            preferred_element_type=jnp.float32,
        )
        * score_scale
    )
    scores = jnp.where(visible[None, None, :], scores, NEG_FLOOR)
    new_max = jnp.maximum(run_max, jnp.max(scores, axis=2))
    probs = jnp.where(visible[None, None, :], jnp.exp(scores - new_max[:, :, None]), 0.0)
    run_total = jnp.sum(probs, axis=2)
    added = jnp.einsum(
        "htk,khd->htd",
        probs.astype(jnp.bfloat16),
        value_part.reshape(piece_rows, heads_here, HD),
        preferred_element_type=jnp.float32,
    )
    run_accum = added
    run_max, run_total, run_accum = (new_max, run_total, run_accum)
    summed = run_accum / run_total[:, :, None]
    attended = (
        jnp.transpose(summed, (1, 0, 2)).reshape(tok_rows, heads_here * HD).astype(jnp.bfloat16)
    )
    projected = jnp.dot(
        attended,
        lax.all_gather(out_weight, "seq", axis=1, tiled=True),
        preferred_element_type=jnp.float32,
    )
    shared = lax.psum_scatter(
        projected.astype(jnp.bfloat16), "head", scatter_dimension=1, tiled=True
    ).astype(jnp.float32)
    my_step = jnp.sum(jnp.where(group_ids == my_span, step_index, 0))
    step_ids = jnp.arange(gate_table.shape[0], dtype=jnp.int32)
    gate_row = jnp.sum(jnp.where((step_ids == my_step)[:, None], gate_table, 0.0), axis=0)
    return (gate_row[None, :] * shared).astype(jnp.bfloat16)


def solution(mesh):
    in_specs = (
        P(("streams", "span", "seq"), "head"),
        P(("streams", "span", "seq"), "head"),
        P(("streams", "span", "seq"), "head"),
        P("head", "seq"),
        P(None, "head"),
        P("streams"),
        P("streams", None),
    )
    out_specs = P(("streams", "span", "seq"), "head")
    return jax.shard_map(
        on_device, mesh=mesh, in_specs=in_specs, out_specs=out_specs, check_vma=False
    )
```

profile of v0, /device:TPU:0, one launch (start us, length us, event | category | flops | bytes accessed | tf_op | source)
XLA Modules:
  0.0 153.1 jit_solution(9862988004682840681)
XLA Ops:
  6.5 0.0 all-gather.6.cloned.1.call-start
  6.5 0.7 all-gather.6.cloned.1.call-update
  7.3 0.0 all-gather.4.cloned.1.call-start
  7.3 1.9 %copy.16 = bf16[256,640]{0,1:T(8,128)(2,1)} copy(bf16[256,640]{1,0:T(8,128)(2,1)} %param.8) | data formatting | bytes 655360 | tf_op args[1]
  9.2 0.0 all-gather.4.cloned.1.call-update
  9.2 0.0 all-gather.8.cloned.1.call-start
  9.2 0.7 all-gather.8.cloned.1.call-update
  9.9 0.0 reduce-scatter.2.cloned.1.call-start
  10.0 1.1 copy.15
  11.2 0.8 select_reduce_fusion.2
  11.9 0.1 select_reduce_fusion.1
  12.0 33.6 %all-gather.6.cloned.1.call-done = bf16[2048,640]{1,0:T(8,128)(2,1)} async-done(((bf16[256,640]{1,0:T(8,128)(2,1)}), bf16[2048,640]{1,0:T(8,128)(2,1)}) %all-gather.6.cloned.1.call-update) | async-done | bytes 2621456 | tf_op jit(solution)/shard_map/all_gather | solution.py:23
  45.6 3.0 %copy.19 = bf16[2048,640]{0,1:T(8,128)(2,1)S(1)} copy(bf16[2048,640]{1,0:T(8,128)(2,1)} %all-gather.6.cloned.1.call-done) | data formatting | bytes 5242880 | tf_op jit(solution)/shard_map/all_gather | solution.py:23
  48.6 32.5 %all-gather.4.cloned.1.call-done = bf16[2048,640]{0,1:T(8,128)(2,1)} async-done(((bf16[256,640]{0,1:T(8,128)(2,1)}), bf16[2048,640]{0,1:T(8,128)(2,1)}) %all-gather.4.cloned.1.call-update) | async-done | bytes 2621456 | tf_op jit(solution)/shard_map/all_gather | solution.py:22
  81.1 3.7 %fusion = (f32[5,256]{1,0:T(8,128)S(1)}, f32[5,256,2048]{2,1,0:T(8,128)S(1)}) fusion(pred[2048]{0:T(1024)(128)(4,1)S(1)} %broadcast_compare_fusion, bf16[256,5,128]{0,2,1:T(8,128)(2,1)S(1)} %bitcast.18, bf16[2048,5,128]{0,2,1:T(8,128)(2,1)} %bitcast.16), kind=kOutput, calls=%fused_computation.2 | convolution fusion | flops 678951680 | bytes 13442048 | tf_op jit(solution)/shard_map/thd,khd->htk/dot_general | solution.py:31
  84.8 2.6 %fusion.1 = f32[5,256]{1,0:T(8,128)S(1)} fusion(f32[5,256,2048]{2,1,0:T(8,128)S(1)} %get-tuple-element.6, f32[5,256]{1,0:T(8,128)S(1)} %broadcast_maximum_fusion, pred[2048]{0:T(1024)(128)(4,1)S(1)} %broadcast_compare_fusion), kind=kLoop, calls=%fused_computation.3 | loop fusion | flops 13105920 | bytes 10498048 | tf_op jit(solution)/shard_map/reduce_sum | solution.py:42
  87.3 3.3 %fusion.12 = bf16[256,5,128]{0,2,1:T(8,128)(2,1)S(1)} fusion(bf16[2048,5,128]{0,2,1:T(8,128)(2,1)S(1)} %bitcast.17, f32[5,256,2048]{2,1,0:T(8,128)S(1)} %get-tuple-element.6, f32[5,256]{1,0:T(8,128)S(1)} %broadcast_maximum_fusion, pred[2048]{0:T(1024)(128)(4,1)S(1)} %broadcast_compare_fusion, f32[256,5]{0,1:T(8,128)S(1)} %bitcast.20), kind=kOutput, calls=%fused_computation.11 | convolution fusion | flops 684523520 | bytes 13447168 | tf_op jit(solution)/shard_map/htk,khd->htd/dot_general | solution.py:43
  90.6 7.7 %all-gather.8.cloned.1.call-done = bf16[640,5120]{1,0:T(8,128)(2,1)} async-done(((bf16[640,2560]{1,0:T(8,128)(2,1)}), bf16[640,5120]{1,0:T(8,128)(2,1)}) %all-gather.8.cloned.1.call-update) | async-done | bytes 6553616 | tf_op jit(solution)/shard_map/all_gather | solution.py:57
  98.4 0.0 copy-start.1
  98.4 0.0 copy-start
  98.4 6.7 %convolution_convert_fusion = bf16[256,5120]{1,0:T(8,128)(2,1)} fusion(bf16[256,640]{0,1:T(8,128)(2,1)S(1)} %bitcast.19, bf16[640,5120]{1,0:T(8,128)(2,1)} %all-gather.8.cloned.1.call-done), kind=kOutput, calls=%fused_computation.5 | convolution fusion | flops 1679032320 | bytes 9502720 | tf_op jit(solution)/shard_map/dot_general | solution.py:55
  105.0 0.0 reduce-scatter.2.cloned.1.call-update
  105.1 0.0 copy-done.1
  105.1 0.6 select_reduce_fusion.3
  105.7 0.6 iota_compare_fusion.2
  106.4 0.0 copy-done
  106.4 0.1 select_reduce_fusion
  106.5 37.5 %reduce-scatter.2.cloned.1.call-done = bf16[256,2560]{1,0:T(8,128)(2,1)} async-done(((bf16[256,5120]{1,0:T(8,128)(2,1)}), bf16[256,2560]{1,0:T(8,128)(2,1)}) %reduce-scatter.2.cloned.1.call-update) | async-done | bytes 1310736 | tf_op jit(solution)/shard_map/reduce_scatter | solution.py:60
  144.0 2.6 %multiply_convert_fusion = bf16[256,2560]{1,0:T(8,128)(2,1)} fusion(bf16[256,2560]{1,0:T(8,128)(2,1)} %reduce-scatter.2.cloned.1.call-done, f32[2560]{0:T(1024)S(1)} %select_reduce_fusion), kind=kLoop, calls=%fused_computation.8 | loop fusion | flops 1966080 | bytes 2631680 | tf_op jit(solution)/shard_map/convert_element_type | solution.py:66
  (4 shorter events, 0.0 us)
Async XLA Ops:
  6.5 39.1 %all-gather.6.cloned.1.call-start = ((), (), s32[]{:S(2)}) async-start(), calls=%async_computation.2 | async-start | bytes 2949120 | tf_op jit(solution)/shard_map/all_gather | solution.py:23
  7.3 73.8 %all-gather.4.cloned.1.call-start = ((), (), s32[]{:S(2)}) async-start(), calls=%async_computation.1 | async-start | bytes 2949120 | tf_op jit(solution)/shard_map/all_gather | solution.py:22
  9.2 89.2 %all-gather.8.cloned.1.call-start = ((), (), s32[]{:S(2)}) async-start(), calls=%async_computation.3 | async-start | bytes 9830400 | tf_op jit(solution)/shard_map/all_gather | solution.py:57
  9.9 134.1 %reduce-scatter.2.cloned.1.call-start = ((), (), s32[]{:S(2)}) async-start(), calls=%async_computation.4 | async-start | bytes 3932160 | tf_op jit(solution)/shard_map/reduce_scatter | solution.py:60
  98.4 6.7 %copy-start.1 = (s32[4]{0:T(128)S(1)}, s32[4]{0:T(128)}, u32[]{:S(2)}) copy-start(s32[4]{0:T(128)} %param.12) | copy-start | bytes 52
  98.4 8.0 %copy-start = (f32[4,2560]{1,0:T(4,128)S(1)}, f32[4,2560]{1,0:T(4,128)}, u32[]{:S(2)}) copy-start(f32[4,2560]{1,0:T(4,128)} %param.11) | copy-start | bytes 122884
Sparse Core Ops, SparseCore 0:
  9.0 36.5 all-gather.5
  47.2 33.8 all-gather.3
  82.6 15.6 all-gather.7
  105.2 38.7 reduce-scatter.1
where the time goes:
time: 153 us
  waiting for transfers between devices  113 us (74%)
  matrix products  13.6 us (9%)
  between operations  13.2 us (9%)
  other arithmetic  7.42 us (5%)
  local copies, waits for them, and re-layouts  6.01 us (4%)
    reduce_scatter x1, waiting for transfers between devices, on_device(): lax.psum_scatter(projected.astype(jnp.bfloat16), 'head', scatter_dimensio...  37.5 us
    all_gather x1, waiting for transfers between devices, on_device(): value_part = lax.all_gather(value_rows, ('span', 'seq'), axis=0, tiled=True)  33.6 us
    all_gather x1, waiting for transfers between devices, on_device(): key_part = lax.all_gather(key_rows, ('span', 'seq'), axis=0, tiled=True)  32.5 us
    all_gather x1, waiting for transfers between devices, on_device(): lax.all_gather(out_weight, 'seq', axis=1, tiled=True)  7.72 us
    dot_general x1, matrix products, on_device(): jnp.dot(attended, lax.all_gather(out_weight, 'seq', axis=1, tiled=True),...  6.68 us
    dot_general x1, matrix products, on_device(): jnp.einsum('thd,khd->htk', query_three, key_part.reshape(piece_rows, head...  3.67 us
    dot_general x1, matrix products, on_device(): jnp.einsum('htk,khd->htd', probs.astype(jnp.bfloat16), value_part.reshape...  3.29 us
  transfers between devices with their start and end apart: 4, of which 4 were waited for; matrix products, arithmetic and copies ran while one was open for 12% of the time, Pallas kernels for 0%

commit v1 on v0

--- a/solution.py
+++ b/solution.py
@@ -19,8 +19,13 @@
     query_three = query_rows.reshape(tok_rows, heads_here, HD)
     score_scale = 1.0 / math.sqrt(HD)
     run_max = jnp.full((heads_here, tok_rows), NEG_FLOOR, jnp.float32)
-    key_part = lax.all_gather(key_rows, ("span", "seq"), axis=0, tiled=True)
-    value_part = lax.all_gather(value_rows, ("span", "seq"), axis=0, tiled=True)
+    key_part, value_part = jnp.split(
+        lax.all_gather(
+            jnp.concatenate([key_rows, value_rows], axis=1), ("span", "seq"), axis=0, tiled=True
+        ),
+        [key_rows.shape[1]],
+        axis=1,
+    )
     piece_rows = key_part.shape[0]
     key_group = jnp.arange(piece_rows, dtype=jnp.int32) // span_tok
     visible = (

time: 153 us -> 141 us (0.922)
  waiting for transfers between devices: 113 us -> 101 us
    all_gather x2 -> x1, waiting for transfers between devices: 66.1 us -> 58.1 us  [on_device(): lax.all_gather(jnp.concatenate([key_rows, value_rows], axis=1), ('span',...]
    split x0 -> x1, local copies, waits for them, and re-layouts: none -> 3.2 us  [on_device(): jnp.split(lax.all_gather(jnp.concatenate([key_rows, value_rows], axis=1),...]
    all_gather x1, waiting for transfers between devices: 7.72 us -> 4.61 us  [on_device(): lax.all_gather(out_weight, 'seq', axis=1, tiled=True)]
    all_gather x1 -> x0, local copies, waits for them, and re-layouts: 2.99 us -> none  [on_device(): value_part = lax.all_gather(value_rows, ('span', 'seq'), axis=0, tiled=True)]
  transfers between devices with their start and end apart: 4 -> 3, of which waited for: 4 -> 3; matrix products, arithmetic and copies ran while one was open for 12% -> 10% of each run, Pallas kernels for 0% -> 0%
where the time goes in v1:
time: 141 us
  waiting for transfers between devices  101 us (72%)
  between operations  13.2 us (9%)
  matrix products  12.5 us (9%)
  other arithmetic  8.25 us (6%)
  local copies, waits for them, and re-layouts  5.73 us (4%)
    all_gather x1, waiting for transfers between devices, on_device(): lax.all_gather(jnp.concatenate([key_rows, value_rows], axis=1), ('span',...  58.1 us
    reduce_scatter x1, waiting for transfers between devices, on_device(): lax.psum_scatter(projected.astype(jnp.bfloat16), 'head', scatter_dimensio...  37.5 us
    dot_general x1, matrix products, on_device(): jnp.dot(attended, lax.all_gather(out_weight, 'seq', axis=1, tiled=True),...  6.68 us
    all_gather x1, waiting for transfers between devices, on_device(): lax.all_gather(out_weight, 'seq', axis=1, tiled=True)  4.61 us
    split x1, local copies, waits for them, and re-layouts, on_device(): jnp.split(lax.all_gather(jnp.concatenate([key_rows, value_rows], axis=1),...  3.2 us
    reduce_sum x1, other arithmetic, on_device(): run_total = jnp.sum(probs, axis=2)  3.2 us
    dot_general x1, matrix products, on_device(): jnp.einsum('thd,khd->htk', query_three, key_part.reshape(piece_rows, head...  3.02 us
    dot_general x1, matrix products, on_device(): jnp.einsum('htk,khd->htd', probs.astype(jnp.bfloat16), value_part.reshape...  2.84 us
  transfers between devices with their start and end apart: 3, of which 3 were waited for; matrix products, arithmetic and copies ran while one was open for 10% of the time, Pallas kernels for 0%

profile of v1, /device:TPU:0, one launch (start us, length us, event | category | flops | bytes accessed | tf_op | source)
XLA Modules:
  0.0 140.8 jit_solution(3415100250800236020)
XLA Ops:
  6.5 0.0 copy-start
  6.5 0.0 copy-start.2
  6.5 0.0 all-gather.3.cloned.1.call-start
  6.5 1.2 copy.18
  7.7 1.1 copy.17
  8.9 0.9 pad_maximum_fusion
  9.8 0.0 all-gather.3.cloned.1.call-update
  9.8 0.0 all-gather.5.cloned.1.call-start
  9.8 0.7 all-gather.5.cloned.1.call-update
  10.5 0.0 reduce-scatter.2.cloned.1.call-start
  10.6 0.0 copy-done
  10.6 0.2 copy.19
  10.8 0.0 copy-done.2
  10.8 0.1 select_reduce_fusion.2
  10.9 0.1 select_reduce_fusion.1
  11.0 58.1 %all-gather.3.cloned.1.call-done = bf16[2048,1280]{0,1:T(8,128)(2,1)} async-done(((bf16[256,1280]{0,1:T(8,128)(2,1)}), bf16[2048,1280]{0,1:T(8,128)(2,1)}) %all-gather.3.cloned.1.call-update) | async-done | bytes 5242896 | tf_op jit(solution)/shard_map/all_gather | solution.py:23
  69.1 3.2 %fusion.23 = (bf16[2048,640]{0,1:T(8,128)(2,1)S(1)}, bf16[2048,640]{0,1:T(8,128)(2,1)S(1)}) fusion(bf16[2048,1280]{0,1:T(8,128)(2,1)} %all-gather.3.cloned.1.call-done), kind=kLoop, calls=%fused_computation.35 | loop fusion | bytes 10485760 | tf_op jit(solution)/shard_map/split | solution.py:22
  72.4 3.0 %bitcast_reduce_fusion = (f32[5,256]{1,0:T(8,128)S(1)}, f32[5,2048,256]{2,1,0:T(8,128)S(1)}) fusion(pred[2048]{0:T(1024)(128)(4,1)S(1)} %broadcast_compare_fusion, bf16[2048,5,128]{0,2,1:T(8,128)(2,1)S(1)} %bitcast.34, bf16[256,5,128]{0,2,1:T(8,128)(2,1)S(1)} %bitcast.36), kind=kOutput, calls=%fused_computation.1 | convolution fusion | flops 678951680 | bytes 13442048 | tf_op jit(solution)/shard_map/thd,khd->htk/dot_general | solution.py:36
  75.4 3.2 %fusion.2 = f32[5,256]{1,0:T(8,128)S(1)} fusion(f32[5,2048,256]{2,1,0:T(8,128)S(1)} %get-tuple-element.8, f32[5,256]{1,0:T(8,128)S(1)} %broadcast_maximum_fusion, pred[2048]{0:T(1024)(128)(4,1)S(1)} %broadcast_compare_fusion), kind=kLoop, calls=%fused_computation.5 | loop fusion | flops 13105920 | bytes 10498048 | tf_op jit(solution)/shard_map/reduce_sum | solution.py:47
  78.6 2.8 %fusion.14 = bf16[256,5,128]{0,2,1:T(8,128)(2,1)S(1)} fusion(bf16[2048,5,128]{0,2,1:T(8,128)(2,1)S(1)} %bitcast.35, f32[5,2048,256]{2,1,0:T(8,128)S(1)} %get-tuple-element.8, f32[5,256]{1,0:T(8,128)S(1)} %broadcast_maximum_fusion, pred[2048]{0:T(1024)(128)(4,1)S(1)} %broadcast_compare_fusion, f32[256,5]{0,1:T(8,128)S(1)} %bitcast.38), kind=kOutput, calls=%fused_computation.14 | convolution fusion | flops 684523520 | bytes 13447168 | tf_op jit(solution)/shard_map/htk,khd->htd/dot_general | solution.py:48
  81.4 4.6 %all-gather.5.cloned.1.call-done = bf16[640,5120]{1,0:T(8,128)(2,1)} async-done(((bf16[640,2560]{1,0:T(8,128)(2,1)}), bf16[640,5120]{1,0:T(8,128)(2,1)}) %all-gather.5.cloned.1.call-update) | async-done | bytes 6553616 | tf_op jit(solution)/shard_map/all_gather | solution.py:62
  86.1 0.0 copy-start.3
  86.1 0.0 copy-start.1
  86.1 6.7 %convolution_convert_fusion = bf16[256,5120]{1,0:T(8,128)(2,1)} fusion(bf16[256,640]{0,1:T(8,128)(2,1)S(1)} %bitcast.37, bf16[640,5120]{1,0:T(8,128)(2,1)} %all-gather.5.cloned.1.call-done), kind=kOutput, calls=%fused_computation.7 | convolution fusion | flops 1679032320 | bytes 9502720 | tf_op jit(solution)/shard_map/dot_general | solution.py:60
  92.7 0.0 reduce-scatter.2.cloned.1.call-update
  92.8 0.0 copy-done.3
  92.8 0.6 select_reduce_fusion.3
  93.4 0.6 iota_compare_fusion.2
  94.1 0.0 copy-done.1
  94.1 0.1 select_reduce_fusion
  94.2 37.5 %reduce-scatter.2.cloned.1.call-done = bf16[256,2560]{1,0:T(8,128)(2,1)} async-done(((bf16[256,5120]{1,0:T(8,128)(2,1)}), bf16[256,2560]{1,0:T(8,128)(2,1)}) %reduce-scatter.2.cloned.1.call-update) | async-done | bytes 1310736 | tf_op jit(solution)/shard_map/reduce_scatter | solution.py:65
  131.7 2.6 %multiply_convert_fusion = bf16[256,2560]{1,0:T(8,128)(2,1)} fusion(bf16[256,2560]{1,0:T(8,128)(2,1)} %reduce-scatter.2.cloned.1.call-done, f32[2560]{0:T(1024)S(1)} %select_reduce_fusion), kind=kLoop, calls=%fused_computation.11 | loop fusion | flops 1966080 | bytes 2631680 | tf_op jit(solution)/shard_map/convert_element_type | solution.py:71
  (4 shorter events, 0.0 us)
Async XLA Ops:
  6.5 4.1 %copy-start = (bf16[256,640]{1,0:T(8,128)(2,1)S(1)}, bf16[256,640]{1,0:T(8,128)(2,1)}, u32[]{:S(2)}) copy-start(bf16[256,640]{1,0:T(8,128)(2,1)} %param.7) | copy-start | bytes 983044
  6.5 4.3 %copy-start.2 = (s32[4,4]{1,0:T(4,128)S(1)}, s32[4,4]{1,0:T(4,128)}, u32[]{:S(2)}) copy-start(s32[4,4]{1,0:T(4,128)} %param.13) | copy-start | bytes 196
  6.5 62.6 %all-gather.3.cloned.1.call-start = ((), (), s32[]{:S(2)}) async-start(), calls=%async_computation.1 | async-start | bytes 5898240 | tf_op jit(solution)/shard_map/all_gather | solution.py:23
  9.8 76.3 %all-gather.5.cloned.1.call-start = ((), (), s32[]{:S(2)}) async-start(), calls=%async_computation.2 | async-start | bytes 9830400 | tf_op jit(solution)/shard_map/all_gather | solution.py:62
  10.5 121.1 %reduce-scatter.2.cloned.1.call-start = ((), (), s32[]{:S(2)}) async-start(), calls=%async_computation.3 | async-start | bytes 3932160 | tf_op jit(solution)/shard_map/reduce_scatter | solution.py:65
  86.1 6.7 %copy-start.3 = (s32[4]{0:T(128)S(1)}, s32[4]{0:T(128)}, u32[]{:S(2)}) copy-start(s32[4]{0:T(128)} %param.12) | copy-start | bytes 52
  86.1 8.0 %copy-start.1 = (f32[4,2560]{1,0:T(4,128)S(1)}, f32[4,2560]{1,0:T(4,128)}, u32[]{:S(2)}) copy-start(f32[4,2560]{1,0:T(4,128)} %param.11) | copy-start | bytes 122884
Sparse Core Ops, SparseCore 0:
  9.9 59.1 all-gather.2
  70.7 15.3 all-gather.4
  92.9 38.7 reduce-scatter.1
